TPU v7x, 32 devices: a whole 2x2x4 slice. The times are simulated.
32 devices in a mesh: blk: 16 (over z, y, x), col: 2 (over core).
Axes of the slice: x: 2, y: 2, z: 4, core: 2. Of those that a mesh axis runs over, the one named last changes fastest.
Arguments:
- queries: bfloat16 [128, 16384], P('blk', 'col'), may hold values from -6 to 6
- factor: bfloat16 [16384, 1024], P('col', 'blk'), may hold values from -0.046875 to 0.046875
- eigenvalues: float32 [1024], replicated, may hold values from 0.05 to 20
- damping: float32 [1], replicated, may hold values from 0.5 to 2
- train_rows: bfloat16 [16384, 16384], P('blk', 'col'), may hold values from -0.046875 to 0.046875
Outputs:
- scores: bfloat16 [128, 16384], P('col', 'blk')
All inputs are finite; a program needn't handle non-finite values.
Results may differ from a plain program's by a relative error of at most 0.0049.
Values may be sent and summed in bfloat16 or wider, within the bound.
A program may use at most 64 MiB of HBM per device.

v0:
```python
import jax
import jax.numpy as jnp
from jax import lax
from jax.sharding import PartitionSpec as P


def row_scores(block_rows, train_rows):
    return jnp.einsum("qk,nk->qn", block_rows, train_rows, preferred_element_type=jnp.float32)


def per_device(queries, factor, eigenvalues, damping, train_rows):
    damp_value = damping[0]
    weights = eigenvalues / (eigenvalues + damp_value)
    rank_slice = factor.shape[1]
    every_query = lax.all_gather(queries, "blk", axis=0, tiled=True)
    partial_value = jnp.dot(every_query, factor, preferred_element_type=jnp.float32)
    coefficient = lax.psum(partial_value, "col")
    slice_weights = lax.dynamic_slice_in_dim(
        weights, lax.axis_index("blk") * rank_slice, rank_slice
    )
    scaled = coefficient * slice_weights[None, :]
    correction_part = jnp.dot(scaled, factor.astype(jnp.float32).T, precision=lax.Precision.HIGHEST)
    correction = lax.psum(correction_part, "blk")
    pre_all = ((every_query.astype(jnp.float32) - correction) / damp_value).astype(jnp.bfloat16)
    partial_scores = row_scores(pre_all, train_rows)
    scores = lax.psum_scatter(partial_scores, "col", scatter_dimension=0, tiled=True)
    return scores.astype(jnp.bfloat16)


def solution(mesh):
    in_specs = (P("blk", "col"), P("col", "blk"), P(), P(), P("blk", "col"))
    out_specs = P("col", "blk")
    return jax.shard_map(
        per_device, mesh=mesh, in_specs=in_specs, out_specs=out_specs, check_vma=False
    )
```

profile of v0, /device:TPU:0, one launch (start us, length us, event | category | flops | bytes accessed | tf_op | source)
XLA Modules:
  0.0 279.0 jit_solution(8576192515819052841)
XLA Ops:
  6.5 0.0 copy-start
  6.5 0.0 all-gather.2.cloned.1.call-start
  6.5 0.7 all-gather.2.cloned.1.call-update
  7.3 0.0 all-reduce.2.cloned.1.call-start
  8.0 0.7 add_divide_fusion
  8.6 0.1 dynamic_slice.3
  8.7 64.5 %all-gather.2.cloned.1.call-done = bf16[128,8192]{1,0:T(8,128)(2,1)} async-done(((bf16[8,8192]{1,0:T(8,128)(2,1)}), bf16[128,8192]{1,0:T(8,128)(2,1)}) %all-gather.2.cloned.1.call-update) | async-done | bytes 2097168 | tf_op jit(solution)/shard_map/all_gather | solution.py:15
  73.2 0.0 copy-done
  73.2 2.3 fusion.5
  75.5 3.6 %psum.14 = f32[128,64]{1,0:T(8,128)S(1)} all-reduce(f32[128,64]{1,0:T(8,128)S(1)} %fusion.5), channel_id=1, replica_groups=mesh['blk'=16,'col'=2] {'col'}, use_global_device_ids=true, to_apply=%region_0.0 | all-reduce | flops 8192 | bytes 65536 | tf_op jit(solution)/shard_map/psum | solution.py:17
  79.1 0.0 copy-start.1
  79.1 3.7 %fusion.2 = f32[128,8192]{1,0:T(8,128)} fusion(bf16[8192,64]{0,1:T(8,128)(2,1)S(1)} %copy-done, f32[128,64]{1,0:T(8,128)S(1)} %psum.14, f32[64]{0:T(128)S(1)} %dynamic_slice.3), kind=kOutput, calls=%fused_computation.3 | convolution fusion | flops 805314560 | bytes 5275904 | tf_op jit(solution)/shard_map/dot_general | solution.py:22
  82.9 0.0 all-reduce.2.cloned.1.call-update
  82.9 0.0 reduce-scatter.2.cloned.1.call-start
  83.0 167.2 %all-reduce.2.cloned.1.call-done = f32[128,8192]{1,0:T(8,128)} async-done(((f32[128,8192]{1,0:T(8,128)}), f32[128,8192]{1,0:T(8,128)}) %all-reduce.2.cloned.1.call-update) | async-done | bytes 4194320 | tf_op jit(solution)/shard_map/psum | solution.py:23
  250.2 0.0 copy-done.1
  250.2 13.5 %fusion = f32[128,1024]{1,0:T(8,128)} fusion(bf16[1024,8192]{1,0:T(8,128)(2,1)} %param.9, f32[128,8192]{1,0:T(8,128)} %all-reduce.2.cloned.1.call-done, bf16[128,8192]{1,0:T(8,128)(2,1)S(1)} %copy-done.1, f32[]{:T(128)} %bitcast.6), kind=kOutput, calls=%fused_computation.1 | convolution fusion | flops 2151677952 | bytes 23592964 | tf_op jit(solution)/shard_map/qk,nk->qn/dot_general | solution.py:8
  263.7 0.0 reduce-scatter.2.cloned.1.call-update
  263.7 7.1 %reduce-scatter.2.cloned.1.call-done = f32[64,1024]{1,0:T(8,128)} async-done(((f32[128,1024]{1,0:T(8,128)}), f32[64,1024]{1,0:T(8,128)}) %reduce-scatter.2.cloned.1.call-update) | async-done | bytes 262160 | tf_op jit(solution)/shard_map/reduce_scatter | solution.py:26
  270.8 1.6 convert_element_type.12
Async XLA Ops:
  6.5 66.7 %copy-start = (bf16[8192,64]{0,1:T(8,128)(2,1)S(1)}, bf16[8192,64]{0,1:T(8,128)(2,1)}, u32[]{:S(2)}) copy-start(bf16[8192,64]{0,1:T(8,128)(2,1)} %param.6) | copy-start | bytes 3145732
  6.5 66.7 %all-gather.2.cloned.1.call-start = ((), (), s32[]{:S(2)}) async-start(), calls=%async_computation.1 | async-start | bytes 2228224 | tf_op jit(solution)/shard_map/all_gather | solution.py:15
  7.3 242.9 %all-reduce.2.cloned.1.call-start = ((), (), s32[]{:S(2)}) async-start(), calls=%async_computation.2 | async-start | bytes 8388608 | tf_op jit(solution)/shard_map/psum | solution.py:23
  79.1 171.0 %copy-start.1 = (bf16[128,8192]{1,0:T(8,128)(2,1)S(1)}, bf16[128,8192]{1,0:T(8,128)(2,1)}, u32[]{:S(2)}) copy-start(bf16[128,8192]{1,0:T(8,128)(2,1)} %all-gather.2.cloned.1.call-done) | copy-start | bytes 6291460
  82.9 187.9 %reduce-scatter.2.cloned.1.call-start = ((), (), s32[]{:S(2)}) async-start(), calls=%async_computation.3 | async-start | bytes 786432 | tf_op jit(solution)/shard_map/reduce_scatter | solution.py:26
Sparse Core Ops, SparseCore 0:
  10.1 63.0 all-gather.1
  83.0 167.0 all-reduce.1
  263.8 6.9 reduce-scatter.1
where the time goes:
time: 279 us
  waiting for transfers between devices  240 us (86%)
  matrix products  19.5 us (7%)
  between operations  13.8 us (5%)
  blocking collectives  3.59 us (1%)
    psum x1, waiting for transfers between devices, per_device(): correction = lax.psum(correction_part, 'blk')  167 us
    all_gather x1, waiting for transfers between devices, per_device(): every_query = lax.all_gather(queries, 'blk', axis=0, tiled=True)  64.5 us
    dot_general x1, matrix products, row_scores(): jnp.einsum('qk,nk->qn', block_rows, train_rows, preferred_element_type=jn...  13.5 us
    reduce_scatter x1, waiting for transfers between devices, per_device(): lax.psum_scatter(partial_scores, 'col', scatter_dimension=0, tiled=True)  7.13 us
  transfers between devices with their start and end apart: 3, of which 3 were waited for; matrix products, arithmetic and copies ran while one was open for 0% of the time, Pallas kernels for 0%

commit v1 on v0

v1 whole, which is shorter than its diff:
```python
import jax
import jax.numpy as jnp
from jax import lax
from jax.sharding import PartitionSpec as P


def per_device(queries, factor, eigenvalues, damping, train_rows):
    damp_value = damping[0]
    weights = eigenvalues / (eigenvalues + damp_value)
    query_part = lax.all_to_all(queries, "blk", split_axis=1, concat_axis=0, tiled=True)
    factor_part = lax.all_to_all(factor, "blk", split_axis=0, concat_axis=1, tiled=True)
    partial_value = jnp.dot(query_part, factor_part, preferred_element_type=jnp.float32)
    coefficient = lax.psum(partial_value, ("blk", "col"))
    scaled = coefficient * weights[None, :]
    correction = jnp.dot(scaled, factor_part.astype(jnp.float32).T, precision=lax.Precision.HIGHEST)
    pre_part = ((query_part.astype(jnp.float32) - correction) / damp_value).astype(jnp.bfloat16)
    pre_all = lax.all_gather(pre_part, "blk", axis=1, tiled=True)
    partial_scores = jnp.einsum("qk,nk->qn", pre_all, train_rows, preferred_element_type=jnp.float32)
    scores = lax.psum_scatter(partial_scores, "col", scatter_dimension=0, tiled=True)
    return scores.astype(jnp.bfloat16)


def solution(mesh):
    in_specs = (P("blk", "col"), P("col", "blk"), P(), P(), P("blk", "col"))
    out_specs = P("col", "blk")
    return jax.shard_map(
        per_device, mesh=mesh, in_specs=in_specs, out_specs=out_specs, check_vma=False
    )
```

time: 279 us -> 270 us (0.968)
  waiting for transfers between devices: 240 us -> 199 us
  blocking collectives: 3.59 us -> 28.3 us
  starting transfers between devices: 0.08 us -> 8.47 us
  matrix products: 19.5 us -> 16.4 us
    psum x1, waiting for transfers between devices: 167 us -> 126 us  [per_device(): coefficient = lax.psum(partial_value, ('blk', 'col'))]
    all_to_all x0 -> x1, blocking collectives: none -> 28.3 us  [per_device(): lax.all_to_all(factor, 'blk', split_axis=0, concat_axis=1, tiled=True)]
    all_to_all x0 -> x1, starting transfers between devices: none -> 8.34 us  [per_device(): lax.all_to_all(queries, 'blk', split_axis=1, concat_axis=0, tiled=True)]
    all_to_all x0 -> x1, waiting for transfers between devices: none -> 6.41 us  [per_device(): lax.all_to_all(queries, 'blk', split_axis=1, concat_axis=0, tiled=True)]
    all_gather x1, waiting for transfers between devices: 64.5 us -> 60.3 us  [per_device(): pre_all = lax.all_gather(pre_part, 'blk', axis=1, tiled=True)]
    psum x1 -> x0, blocking collectives: 3.59 us -> none  [per_device(): coefficient = lax.psum(partial_value, 'col')]
    dot_general x3, matrix products: 19.5 us -> 16.4 us  [the longest x1 12.9 us: per_device(): jnp.einsum('qk,nk->qn', pre_all, train_rows, preferred_element_type=jnp.f...]
  transfers between devices with their start and end apart: 3 -> 4, of which waited for: 3 -> 4; matrix products, arithmetic and copies ran while one was open for 0% -> 1% of each run, Pallas kernels for 0% -> 0%
where the time goes in v1:
time: 270 us
  waiting for transfers between devices  199 us (74%)
  blocking collectives  28.3 us (10%)
  matrix products  16.4 us (6%)
  between operations  13.8 us (5%)
  starting transfers between devices  8.47 us (3%)
    psum x1, waiting for transfers between devices, per_device(): coefficient = lax.psum(partial_value, ('blk', 'col'))  126 us
    all_gather x1, waiting for transfers between devices, per_device(): pre_all = lax.all_gather(pre_part, 'blk', axis=1, tiled=True)  60.3 us
    all_to_all x1, blocking collectives, per_device(): lax.all_to_all(factor, 'blk', split_axis=0, concat_axis=1, tiled=True)  28.3 us
    dot_general x1, matrix products, per_device(): jnp.einsum('qk,nk->qn', pre_all, train_rows, preferred_element_type=jnp.f...  12.9 us
    all_to_all x1, starting transfers between devices, per_device(): lax.all_to_all(queries, 'blk', split_axis=1, concat_axis=0, tiled=True)  8.34 us
    all_to_all x1, waiting for transfers between devices, per_device(): lax.all_to_all(queries, 'blk', split_axis=1, concat_axis=0, tiled=True)  6.41 us
    reduce_scatter x1, waiting for transfers between devices, per_device(): lax.psum_scatter(partial_scores, 'col', scatter_dimension=0, tiled=True)  6.26 us
  transfers between devices with their start and end apart: 4, of which 4 were waited for; matrix products, arithmetic and copies ran while one was open for 1% of the time, Pallas kernels for 0%

profile of v1, /device:TPU:0, one launch (start us, length us, event | category | flops | bytes accessed | tf_op | source)
XLA Modules:
  0.0 269.8 jit_solution(12998497539709083565)
XLA Ops:
  6.5 8.3 %all-to-all-start = ((bf16[8,16,512]{2,0,1:T(8,128)(2,1)}), bf16[8,16,512]{2,0,1:T(8,128)(2,1)S(1)}, u32[]{:S(2)}, u32[]{:S(2)}) async-start(bf16[8,16,512]{2,0,1:T(8,128)(2,1)} %bitcast.25), calls=%async_computation | async-start | bytes 262144 | tf_op jit(solution)/shard_map/all_to_all | solution.py:10
  14.9 0.0 all-reduce.2.cloned.1.call-start
  14.9 1.3 copy.10
  16.3 6.4 %all-to-all-done = bf16[8,16,512]{2,0,1:T(8,128)(2,1)S(1)} async-done(((bf16[8,16,512]{2,0,1:T(8,128)(2,1)}), bf16[8,16,512]{2,0,1:T(8,128)(2,1)S(1)}, u32[]{:S(2)}, u32[]{:S(2)}) %all-to-all-start) | async-done | bytes 131104 | tf_op jit(solution)/shard_map/all_to_all | solution.py:10
  22.7 28.3 %all_to_all.38 = bf16[16,512,64]{1,2,0:T(8,128)(2,1)S(1)} all-to-all(bf16[16,512,64]{1,2,0:T(8,128)(2,1)S(1)} %bitcast.21), channel_id=1, replica_groups=mesh['blk'=16,'col'=2] {'blk'}, dimensions={0} | all-to-all | bytes 2097152 | tf_op jit(solution)/shard_map/all_to_all | solution.py:11
  51.0 1.3 fusion.4
  52.3 0.0 all-reduce.2.cloned.1.call-update
  52.3 0.0 all-gather.2.cloned.1.call-start
  53.0 0.7 add_divide_fusion
  53.7 126.2 %all-reduce.2.cloned.1.call-done = f32[128,1024]{1,0:T(8,128)} async-done(((f32[128,1024]{1,0:T(8,128)}), f32[128,1024]{1,0:T(8,128)}) %all-reduce.2.cloned.1.call-update) | async-done | bytes 524304 | tf_op jit(solution)/shard_map/psum | solution.py:13
  179.9 2.3 fusion.1
  182.2 0.0 all-gather.2.cloned.1.call-update
  182.2 0.0 reduce-scatter.2.cloned.1.call-start
  182.2 60.3 %all-gather.2.cloned.1.call-done = bf16[128,8192]{1,0:T(8,128)(2,1)} async-done(((bf16[128,512]{1,0:T(8,128)(2,1)}), bf16[128,8192]{1,0:T(8,128)(2,1)}) %all-gather.2.cloned.1.call-update) | async-done | bytes 2097168 | tf_op jit(solution)/shard_map/all_gather | solution.py:17
  242.5 12.9 %fusion.6 = f32[128,1024]{1,0:T(8,128)} fusion(bf16[128,8192]{1,0:T(8,128)(2,1)} %all-gather.2.cloned.1.call-done, bf16[1024,8192]{1,0:T(8,128)(2,1)} %param.9), kind=kOutput, calls=%fused_computation.9 | convolution fusion | flops 2147483648 | bytes 19398656 | tf_op jit(solution)/shard_map/qk,nk->qn/dot_general | solution.py:18
  255.4 0.0 reduce-scatter.2.cloned.1.call-update
  255.4 6.3 %reduce-scatter.2.cloned.1.call-done = f32[64,1024]{1,0:T(8,128)} async-done(((f32[128,1024]{1,0:T(8,128)}), f32[64,1024]{1,0:T(8,128)}) %reduce-scatter.2.cloned.1.call-update) | async-done | bytes 262160 | tf_op jit(solution)/shard_map/reduce_scatter | solution.py:19
  261.7 1.6 convert_element_type.12
Async XLA Ops:
  6.5 16.1 %all-to-all-start = ((bf16[8,16,512]{2,0,1:T(8,128)(2,1)}), bf16[8,16,512]{2,0,1:T(8,128)(2,1)S(1)}, u32[]{:S(2)}, u32[]{:S(2)}) async-start(bf16[8,16,512]{2,0,1:T(8,128)(2,1)} %bitcast.25), calls=%async_computation | async-start | bytes 262144 | tf_op jit(solution)/shard_map/all_to_all | solution.py:10
  14.9 165.0 %all-reduce.2.cloned.1.call-start = ((), (), s32[]{:S(2)}) async-start(), calls=%async_computation.3 | async-start | bytes 1048576 | tf_op jit(solution)/shard_map/psum | solution.py:13
  52.3 190.2 %all-gather.2.cloned.1.call-start = ((), (), s32[]{:S(2)}) async-start(), calls=%async_computation.4 | async-start | bytes 2228224 | tf_op jit(solution)/shard_map/all_gather | solution.py:17
  182.2 79.5 %reduce-scatter.2.cloned.1.call-start = ((), (), s32[]{:S(2)}) async-start(), calls=%async_computation.5 | async-start | bytes 786432 | tf_op jit(solution)/shard_map/reduce_scatter | solution.py:19
Sparse Core Ops, SparseCore 0:
  52.4 127.3 all-reduce.1
  182.6 59.8 all-gather.1
  255.6 6.0 reduce-scatter.1

commit v2 on v1

--- a/solution.py
+++ b/solution.py
@@ -1,10 +1,205 @@
+import functools
+
 import jax
 import jax.numpy as jnp
 from jax import lax
+from jax.experimental import pallas as pl
+from jax.experimental.pallas import tpu as pltpu
 from jax.sharding import PartitionSpec as P
 
-
-def per_device(queries, factor, eigenvalues, damping, train_rows):
+MESH = pl.DeviceIdType.MESH
+CONTRACT_LAST = (((1,), (1,)), ((), ()))
+
+
+def fused_kernel(
+    nb, queries, factor_t, eigenvalues, damping, train_rows, out,
+    query_in, factor_in, train_in, part, part_in, half_sum, half_in, scaled_out, scaled_in,
+    pre, total, total_in,
+    train_sem, own_sem, query_send, query_recv, factor_send, factor_recv,
+    part_send, part_recv, scaled_send, scaled_recv, pre_send, pre_recv, pair_send, pair_recv,
+):
+    me = lax.axis_index("blk")
+    side = lax.axis_index("col")
+    rows, width = query_in.shape[1], query_in.shape[2]
+    rank = eigenvalues.shape[1]
+    every = nb * rows
+    half = every // 2
+
+    def span(index):
+        return pl.ds(pl.multiple_of(index * width, width), width)
+
+    def to_peer(source, target, send_sem, recv_sem, peer):
+        return pltpu.make_async_remote_copy(
+            src_ref=source, dst_ref=target, send_sem=send_sem, recv_sem=recv_sem,
+            device_id={"blk": peer}, device_id_type=MESH,
+        )
+
+    def to_pair(source, target, index):
+        return pltpu.make_async_remote_copy(
+            src_ref=source, dst_ref=target,
+            send_sem=pair_send.at[index], recv_sem=pair_recv.at[index],
+            device_id={"col": 1 - side}, device_id_type=MESH,
+        )
+
+    def each_peer(body):
+        def step(k, carry):
+            body(lax.rem(me + k, nb))
+            return carry
+        lax.fori_loop(1, nb, step, 0)
+
+    def query_copy(source, peer):
+        return to_peer(queries.at[:, span(peer)], query_in.at[source],
+                       query_send.at[peer], query_recv.at[source], peer)
+
+    def factor_copy(source, peer):
+        return to_peer(factor_t.at[:, span(peer)], factor_in.at[source],
+                       factor_send.at[peer], factor_recv.at[source], peer)
+
+    def part_copy(source, peer):
+        return to_peer(part.at[peer], part_in.at[source],
+                       part_send.at[peer], part_recv.at[source], peer)
+
+    def scaled_copy(source, peer):
+        return to_peer(scaled_out, scaled_in.at[source],
+                       scaled_send.at[peer], scaled_recv.at[source], peer)
+
+    def pre_copy(source, peer):
+        return to_peer(pre.at[source], pre.at[source],
+                       pre_send.at[peer], pre_recv.at[source], peer)
+
+    def train_copy(index):
+        return pltpu.make_async_copy(
+            train_rows.at[:, span(index)], train_in.at[index], train_sem.at[index])
+
+    own_query = pltpu.make_async_copy(queries.at[:, span(me)], query_in.at[me], own_sem.at[0])
+    own_factor = pltpu.make_async_copy(factor_t.at[:, span(me)], factor_in.at[me], own_sem.at[1])
+
+    barrier = pltpu.get_barrier_semaphore()
+    each_peer(lambda peer: pl.semaphore_signal(
+        barrier, inc=1, device_id={"blk": peer}, device_id_type=MESH))
+    pl.semaphore_signal(barrier, inc=1, device_id={"col": 1 - side}, device_id_type=MESH)
+    pl.semaphore_wait(barrier, nb)
+
+    own_query.start()
+    own_factor.start()
+    each_peer(lambda peer: query_copy(me, peer).start())
+    each_peer(lambda peer: factor_copy(me, peer).start())
+
+    def start_train(k, carry):
+        train_copy(lax.rem(me + nb - k, nb)).start()
+        return carry
+    lax.fori_loop(0, nb, start_train, 0)
+
+    own_query.wait()
+    own_factor.wait()
+    each_peer(lambda peer: query_copy(peer, peer).wait_recv())
+    each_peer(lambda peer: factor_copy(peer, peer).wait_recv())
+
+    query_wide = query_in[...].astype(jnp.float32).reshape(every, width)
+    factor_slice = factor_in[...].reshape(rank, width)
+    partial_value = lax.dot_general(
+        query_wide.astype(jnp.bfloat16), factor_slice, CONTRACT_LAST,
+        preferred_element_type=jnp.float32)
+    part[...] = partial_value.reshape(nb, rows, rank)
+
+    each_peer(lambda peer: part_copy(me, peer).start())
+    part_in[me] = part[me]
+    each_peer(lambda peer: part_copy(peer, peer).wait_recv())
+    half_sum[...] = jnp.sum(part_in[...], axis=0)
+    exchange = to_pair(half_sum, half_in, 0)
+    exchange.start()
+    weights = eigenvalues[...] / (eigenvalues[...] + damping[0])
+    exchange.wait()
+    scaled_out[...] = (half_sum[...] + half_in[...]) * weights
+    each_peer(lambda peer: scaled_copy(me, peer).start())
+    scaled_in[me] = scaled_out[...]
+    each_peer(lambda peer: scaled_copy(peer, peer).wait_recv())
+
+    scaled = scaled_in[...].reshape(every, rank)
+    first = scaled.astype(jnp.bfloat16)
+    rest = scaled - first.astype(jnp.float32)
+    second = rest.astype(jnp.bfloat16)
+    third = (rest - second.astype(jnp.float32)).astype(jnp.bfloat16)
+    factor_slice = factor_in[...].reshape(rank, width)
+    correction = (
+        jnp.dot(third, factor_slice, preferred_element_type=jnp.float32)
+        + jnp.dot(second, factor_slice, preferred_element_type=jnp.float32)
+    ) + jnp.dot(first, factor_slice, preferred_element_type=jnp.float32)
+    query_wide = query_in[...].astype(jnp.float32).reshape(every, width)
+    pre[me] = ((query_wide - correction) / damping[0]).astype(jnp.bfloat16)
+
+    each_peer(lambda peer: pre_copy(me, peer).start())
+
+    def scores_of(index):
+        train_copy(index).wait()
+        return lax.dot_general(
+            pre[index], train_in[index], CONTRACT_LAST, preferred_element_type=jnp.float32)
+
+    total[...] = scores_of(me)
+
+    def score_step(k, carry):
+        source = lax.rem(me + nb - k, nb)
+        pre_copy(source, source).wait_recv()
+        total[...] += scores_of(source)
+        return carry
+    lax.fori_loop(1, nb, score_step, 0)
+
+    other_rows = pl.ds(pl.multiple_of((1 - side) * half, half), half)
+    own_rows = pl.ds(pl.multiple_of(side * half, half), half)
+    last = to_pair(total.at[other_rows], total_in, 1)
+    last.start()
+
+    def finish(peer):
+        query_copy(me, peer).wait_send()
+        factor_copy(me, peer).wait_send()
+        part_copy(me, peer).wait_send()
+        scaled_copy(me, peer).wait_send()
+        pre_copy(me, peer).wait_send()
+    each_peer(finish)
+    last.wait()
+    out[...] = (total[own_rows, :] + total_in[...]).astype(out.dtype)
+
+
+def fused(nb, queries, factor, eigenvalues, damping, train_rows):
+    rows, depth = queries.shape
+    rank_slice = factor.shape[1]
+    width = depth // nb
+    rank = eigenvalues.shape[0]
+    every = nb * rows
+    train = train_rows.shape[0]
+    anywhere = pl.BlockSpec(memory_space=pl.ANY)
+    vmem = pl.BlockSpec(memory_space=pltpu.VMEM)
+    dma = pltpu.SemaphoreType.DMA
+    f32, bf16 = jnp.float32, jnp.bfloat16
+    return pl.pallas_call(
+        functools.partial(fused_kernel, nb),
+        out_shape=jax.ShapeDtypeStruct((every // 2, train), bf16),
+        in_specs=[anywhere, anywhere, vmem, pl.BlockSpec(memory_space=pltpu.SMEM), anywhere],
+        out_specs=vmem,
+        scratch_shapes=[
+            pltpu.VMEM((nb, rows, width), bf16),
+            pltpu.VMEM((nb, rank_slice, width), bf16),
+            pltpu.VMEM((nb, train, width), bf16),
+            pltpu.VMEM((nb, rows, rank), f32),
+            pltpu.VMEM((nb, rows, rank), f32),
+            pltpu.VMEM((rows, rank), f32),
+            pltpu.VMEM((rows, rank), f32),
+            pltpu.VMEM((rows, rank), f32),
+            pltpu.VMEM((nb, rows, rank), f32),
+            pltpu.VMEM((nb, every, width), bf16),
+            pltpu.VMEM((every, train), f32),
+            pltpu.VMEM((every // 2, train), f32),
+            dma((nb,)), dma((2,)),
+            dma((nb,)), dma((nb,)), dma((nb,)), dma((nb,)),
+            dma((nb,)), dma((nb,)), dma((nb,)), dma((nb,)),
+            dma((nb,)), dma((nb,)), dma((2,)), dma((2,)),
+        ],
+        compiler_params=pltpu.CompilerParams(
+            collective_id=0, has_side_effects=True, vmem_limit_bytes=56 * 1024 * 1024),
+    )(queries, factor.T, eigenvalues[None, :], damping, train_rows)
+
+
+def plain(queries, factor, eigenvalues, damping, train_rows):
     damp_value = damping[0]
     weights = eigenvalues / (eigenvalues + damp_value)
     query_part = lax.all_to_all(queries, "blk", split_axis=1, concat_axis=0, tiled=True)
@@ -20,9 +215,19 @@
     return scores.astype(jnp.bfloat16)
 
 
+def per_device(nb, pair, queries, factor, eigenvalues, damping, train_rows):
+    rows, depth = queries.shape
+    width = depth // nb
+    fits = pair == 2 and width % 128 == 0 and rows % 8 == 0 and factor.shape[1] % 16 == 0
+    if fits:
+        return fused(nb, queries, factor, eigenvalues, damping, train_rows)
+    return plain(queries, factor, eigenvalues, damping, train_rows)
+
+
 def solution(mesh):
     in_specs = (P("blk", "col"), P("col", "blk"), P(), P(), P("blk", "col"))
     out_specs = P("col", "blk")
+    body = functools.partial(per_device, mesh.shape["blk"], mesh.shape["col"])
     return jax.shard_map(
-        per_device, mesh=mesh, in_specs=in_specs, out_specs=out_specs, check_vma=False
+        body, mesh=mesh, in_specs=in_specs, out_specs=out_specs, check_vma=False
     )

time: 270 us -> 121 us (0.45)
  the two profiles are of different devices: /device:TPU:0 before, /device:TPU:31 now
where the time goes in v2:
time: 121 us
  Pallas kernels  119 us (98%)
  local copies, waits for them, and re-layouts  1.57 us (1%)
    pallas_call x1, Pallas kernels, fused(): pl.pallas_call(functools.partial(fused_kernel, nb), out_shape=jax.ShapeDt...  119 us

profile of v2, /device:TPU:31, one launch (start us, length us, event | category | flops | bytes accessed | tf_op | source)
XLA Modules:
  0.0 121.0 jit_solution(8363723391929572559)
XLA Ops:
  0.7 118.8 %shard_map.55 = bf16[64,1024]{1,0:T(8,128)(2,1)} custom-call(bf16[8,8192]{1,0:T(8,128)(2,1)} %queries.1, bf16[64,8192]{1,0:T(8,128)(2,1)} %bitcast.2, f32[1,1024]{1,0:T(1,128)} %bitcast.3, f32[1]{0:T(128)S(6)} %copy.7.damping, bf16[1024,8192]{1,0:T(8,128)(2,1)} %train_rows.1), custom_call_target="tpu_custom_call" | custom-call | tf_op jit(solution)/shard_map/pallas_call | solution.py:174
  119.4 1.6 %copy.8 = bf16[64,1024]{1,0:T(8,128)(2,1)} copy(bf16[64,1024]{1,0:T(8,128)(2,1)} %shard_map.55) | data formatting | bytes 262144

commit v3 on v2

--- a/solution.py
+++ b/solution.py
@@ -13,10 +13,11 @@
 
 def fused_kernel(
     nb, queries, factor_t, eigenvalues, damping, train_rows, out,
-    query_in, factor_in, train_in, part, part_in, half_sum, half_in, scaled_out, scaled_in,
+    query_in, factor_in, train_in, part, pair_in, part_sum, part_in, scaled_out, scaled_in,
     pre, total, total_in,
     train_sem, own_sem, query_send, query_recv, factor_send, factor_recv,
-    part_send, part_recv, scaled_send, scaled_recv, pre_send, pre_recv, pair_send, pair_recv,
+    part_send, part_recv, scaled_send, scaled_recv, line_send, line_recv,
+    side_send, side_recv, corner_send, corner_recv, pair_send, pair_recv,
 ):
     me = lax.axis_index("blk")
     side = lax.axis_index("col")
@@ -24,6 +25,11 @@
     rank = eigenvalues.shape[1]
     every = nb * rows
     half = every // 2
+    half_rank = rank // 2
+    line = nb // 4
+    px, py, pz = lax.rem(me, 2), lax.rem(lax.div(me, 2), 2), lax.div(me, 4)
+    next_x = me + 1 - 2 * px
+    next_y = me + 2 - 4 * py
 
     def span(index):
         return pl.ds(pl.multiple_of(index * width, width), width)
@@ -56,16 +62,33 @@
                        factor_send.at[peer], factor_recv.at[source], peer)
 
     def part_copy(source, peer):
-        return to_peer(part.at[peer], part_in.at[source],
+        return to_peer(part_sum.at[peer], part_in.at[source],
                        part_send.at[peer], part_recv.at[source], peer)
 
     def scaled_copy(source, peer):
-        return to_peer(scaled_out, scaled_in.at[source],
+        return to_peer(scaled_out, scaled_in.at[side, source],
                        scaled_send.at[peer], scaled_recv.at[source], peer)
 
-    def pre_copy(source, peer):
-        return to_peer(pre.at[source], pre.at[source],
-                       pre_send.at[peer], pre_recv.at[source], peer)
+    def block(z, flip_x, flip_y):
+        x = 1 - px if flip_x else px
+        y = 1 - py if flip_y else py
+        return z * 4 + y * 2 + x
+
+    def line_copy(z, up):
+        index = block(z, False, False)
+        return to_peer(pre.at[index], pre.at[index], line_send.at[up, z], line_recv.at[z],
+                       me + (4 if up else -4))
+
+    def side_copy(z, along, incoming=False):
+        index = block(z, incoming and along == 0, incoming and along == 1)
+        return to_peer(pre.at[index], pre.at[index], side_send.at[along, z],
+                       side_recv.at[along, z], next_y if along else next_x)
+
+    def corner_copy(z, along, incoming=False):
+        index = block(z, incoming or along == 1, incoming or along == 0)
+        rows_of = pl.ds((1 - along) * half, half)
+        return to_peer(pre.at[index, rows_of], pre.at[index, rows_of], corner_send.at[along, z],
+                       corner_recv.at[along, z], next_y if along else next_x)
 
     def train_copy(index):
         return pltpu.make_async_copy(
@@ -100,49 +123,87 @@
     partial_value = lax.dot_general(
         query_wide.astype(jnp.bfloat16), factor_slice, CONTRACT_LAST,
         preferred_element_type=jnp.float32)
-    part[...] = partial_value.reshape(nb, rows, rank)
-
+    for k in range(2):
+        part[k] = partial_value[:, k * half_rank:(k + 1) * half_rank].reshape(nb, rows, half_rank)
+
+    exchange = to_pair(part.at[1 - side], pair_in, 0)
+    exchange.start()
+    own_rank = pl.ds(pl.multiple_of(side * half_rank, half_rank), half_rank)
+    own_values = eigenvalues[:, own_rank]
+    weights = own_values / (own_values + damping[0])
+    exchange.wait()
+    part_sum[...] = part[side] + pair_in[...]
     each_peer(lambda peer: part_copy(me, peer).start())
-    part_in[me] = part[me]
+    part_in[me] = part_sum[me]
     each_peer(lambda peer: part_copy(peer, peer).wait_recv())
-    half_sum[...] = jnp.sum(part_in[...], axis=0)
-    exchange = to_pair(half_sum, half_in, 0)
-    exchange.start()
-    weights = eigenvalues[...] / (eigenvalues[...] + damping[0])
-    exchange.wait()
-    scaled_out[...] = (half_sum[...] + half_in[...]) * weights
+    scaled_out[...] = jnp.sum(part_in[...], axis=0) * weights
     each_peer(lambda peer: scaled_copy(me, peer).start())
-    scaled_in[me] = scaled_out[...]
+    scaled_in[side, me] = scaled_out[...]
     each_peer(lambda peer: scaled_copy(peer, peer).wait_recv())
-
-    scaled = scaled_in[...].reshape(every, rank)
-    first = scaled.astype(jnp.bfloat16)
-    rest = scaled - first.astype(jnp.float32)
-    second = rest.astype(jnp.bfloat16)
-    third = (rest - second.astype(jnp.float32)).astype(jnp.bfloat16)
-    factor_slice = factor_in[...].reshape(rank, width)
-    correction = (
-        jnp.dot(third, factor_slice, preferred_element_type=jnp.float32)
-        + jnp.dot(second, factor_slice, preferred_element_type=jnp.float32)
-    ) + jnp.dot(first, factor_slice, preferred_element_type=jnp.float32)
+    swap = to_pair(scaled_in.at[side], scaled_in.at[side], 2)
+    swap.start()
+
+    def correction_of(which):
+        scaled = scaled_in[which].reshape(every, half_rank)
+        first = scaled.astype(jnp.bfloat16)
+        rest = scaled - first.astype(jnp.float32)
+        second = rest.astype(jnp.bfloat16)
+        third = (rest - second.astype(jnp.float32)).astype(jnp.bfloat16)
+        slots = nb // 2
+        factor_half = factor_in[pl.ds(which * slots, slots)].reshape(half_rank, width)
+        return (
+            jnp.dot(third, factor_half, preferred_element_type=jnp.float32)
+            + jnp.dot(second, factor_half, preferred_element_type=jnp.float32)
+        ) + jnp.dot(first, factor_half, preferred_element_type=jnp.float32)
+
+    correction = correction_of(side)
+    swap.wait()
+    correction = correction + correction_of(1 - side)
     query_wide = query_in[...].astype(jnp.float32).reshape(every, width)
     pre[me] = ((query_wide - correction) / damping[0]).astype(jnp.bfloat16)
-
-    each_peer(lambda peer: pre_copy(me, peer).start())
 
     def scores_of(index):
         train_copy(index).wait()
         return lax.dot_general(
             pre[index], train_in[index], CONTRACT_LAST, preferred_element_type=jnp.float32)
 
-    total[...] = scores_of(me)
-
-    def score_step(k, carry):
-        source = lax.rem(me + nb - k, nb)
-        pre_copy(source, source).wait_recv()
-        total[...] += scores_of(source)
-        return carry
-    lax.fori_loop(1, nb, score_step, 0)
+    def height(i):
+        mirror = lax.div(pz, line // 2)
+        near = pz + mirror * (line - 1 - 2 * pz)
+        v = near + i * (1 - 2 * near) if i < 2 else i
+        return v + mirror * (line - 1 - 2 * v)
+
+    def pass_on(z):
+        @pl.when((z <= pz) & (pz < line - 1))
+        def _():
+            line_copy(z, 1).start()
+
+        @pl.when((z >= pz) & (pz > 0))
+        def _():
+            line_copy(z, 0).start()
+
+    total[...] = jnp.zeros_like(total)
+    for i in range(line + 2):
+        if i < line:
+            z = height(i)
+            if i > 0:
+                line_copy(z, 1).wait_recv()
+            pass_on(z)
+            side_copy(z, 0).start()
+            side_copy(z, 1).start()
+        if 1 <= i <= line:
+            z = height(i - 1)
+            side_copy(z, 0, True).wait_recv()
+            corner_copy(z, 1).start()
+            side_copy(z, 1, True).wait_recv()
+            corner_copy(z, 0).start()
+        if i >= 2:
+            z = height(i - 2)
+            corner_copy(z, 0, True).wait_recv()
+            corner_copy(z, 1, True).wait_recv()
+            for flip_x in (False, True):
+                for flip_y in (False, True):
+                    total[...] += scores_of(block(z, flip_x, flip_y))
 
     other_rows = pl.ds(pl.multiple_of((1 - side) * half, half), half)
     own_rows = pl.ds(pl.multiple_of(side * half, half), half)
@@ -154,8 +215,21 @@
         factor_copy(me, peer).wait_send()
         part_copy(me, peer).wait_send()
         scaled_copy(me, peer).wait_send()
-        pre_copy(me, peer).wait_send()
     each_peer(finish)
+    for i in range(line):
+        z = height(i)
+
+        @pl.when((z <= pz) & (pz < line - 1))
+        def _():
+            line_copy(z, 1).wait_send()
+
+        @pl.when((z >= pz) & (pz > 0))
+        def _():
+            line_copy(z, 0).wait_send()
+
+        for along in range(2):
+            side_copy(z, along).wait_send()
+            corner_copy(z, along).wait_send()
     last.wait()
     out[...] = (total[own_rows, :] + total_in[...]).astype(out.dtype)
 
@@ -167,6 +241,7 @@
     rank = eigenvalues.shape[0]
     every = nb * rows
     train = train_rows.shape[0]
+    line = nb // 4
     anywhere = pl.BlockSpec(memory_space=pl.ANY)
     vmem = pl.BlockSpec(memory_space=pltpu.VMEM)
     dma = pltpu.SemaphoreType.DMA
@@ -180,19 +255,20 @@
             pltpu.VMEM((nb, rows, width), bf16),
             pltpu.VMEM((nb, rank_slice, width), bf16),
             pltpu.VMEM((nb, train, width), bf16),
-            pltpu.VMEM((nb, rows, rank), f32),
-            pltpu.VMEM((nb, rows, rank), f32),
-            pltpu.VMEM((rows, rank), f32),
-            pltpu.VMEM((rows, rank), f32),
-            pltpu.VMEM((rows, rank), f32),
-            pltpu.VMEM((nb, rows, rank), f32),
+            pltpu.VMEM((2, nb, rows, rank // 2), f32),
+            pltpu.VMEM((nb, rows, rank // 2), f32),
+            pltpu.VMEM((nb, rows, rank // 2), f32),
+            pltpu.VMEM((nb, rows, rank // 2), f32),
+            pltpu.VMEM((rows, rank // 2), f32),
+            pltpu.VMEM((2, nb, rows, rank // 2), f32),
             pltpu.VMEM((nb, every, width), bf16),
             pltpu.VMEM((every, train), f32),
             pltpu.VMEM((every // 2, train), f32),
             dma((nb,)), dma((2,)),
             dma((nb,)), dma((nb,)), dma((nb,)), dma((nb,)),
             dma((nb,)), dma((nb,)), dma((nb,)), dma((nb,)),
-            dma((nb,)), dma((nb,)), dma((2,)), dma((2,)),
+            dma((2, line)), dma((line,)), dma((2, line)), dma((2, line)),
+            dma((2, line)), dma((2, line)), dma((3,)), dma((3,)),
         ],
         compiler_params=pltpu.CompilerParams(
             collective_id=0, has_side_effects=True, vmem_limit_bytes=56 * 1024 * 1024),
@@ -219,6 +295,7 @@
     rows, depth = queries.shape
     width = depth // nb
     fits = pair == 2 and width % 128 == 0 and rows % 8 == 0 and factor.shape[1] % 16 == 0
+    fits = fits and nb == 16
     if fits:
         return fused(nb, queries, factor, eigenvalues, damping, train_rows)
     return plain(queries, factor, eigenvalues, damping, train_rows)

time: 121 us -> 87.2 us (0.72)
  the two profiles are of different devices: /device:TPU:31 before, /device:TPU:0 now
where the time goes in v3:
time: 87.2 us; the launch traced here: 87 us
  Pallas kernels  84.7 us (97%)
  local copies, waits for them, and re-layouts  1.57 us (2%)
    pallas_call x1, Pallas kernels, fused(): pl.pallas_call(functools.partial(fused_kernel, nb), out_shape=jax.ShapeDt...  84.7 us

profile of v3, /device:TPU:0, one launch (start us, length us, event | category | flops | bytes accessed | tf_op | source)
XLA Modules:
  0.0 87.0 jit_solution(15943946015244855793)
XLA Ops:
  0.7 84.7 %shard_map.55 = bf16[64,1024]{1,0:T(8,128)(2,1)} custom-call(bf16[8,8192]{1,0:T(8,128)(2,1)} %queries.1, bf16[64,8192]{1,0:T(8,128)(2,1)} %bitcast.2, f32[1,1024]{1,0:T(1,128)} %bitcast.3, f32[1]{0:T(128)S(6)} %copy.7.damping, bf16[1024,8192]{1,0:T(8,128)(2,1)} %train_rows.1), custom_call_target="tpu_custom_call" | custom-call | tf_op jit(solution)/shard_map/pallas_call | solution.py:249
  85.4 1.6 %copy.8 = bf16[64,1024]{1,0:T(8,128)(2,1)} copy(bf16[64,1024]{1,0:T(8,128)(2,1)} %shard_map.55) | data formatting | bytes 262144

commit v4 on v3

v4 whole, which is shorter than its diff:
```python
import functools

import jax
import jax.numpy as jnp
from jax import lax
from jax.experimental import pallas as pl
from jax.experimental.pallas import tpu as pltpu
from jax.sharding import PartitionSpec as P

MESH = pl.DeviceIdType.MESH
CONTRACT_LAST = (((1,), (1,)), ((), ()))


def fused_kernel(
    nb, queries, factor_t, eigenvalues, damping, train_rows, out,
    query_in, factor_in, train_in, part, pair_in, part_sum, part_in, scaled_out, scaled_in,
    cross_out, cross_in, pre, total, total_in,
    train_sem, own_sem, query_send, query_recv, factor_send, factor_recv,
    part_send, part_recv, scaled_send, scaled_recv, line_send, line_recv,
    side_send, side_recv, corner_send, corner_recv, pair_send, pair_recv, cross_send, cross_recv,
):
    me = lax.axis_index("blk")
    side = lax.axis_index("col")
    rows, wide = query_in.shape[1], query_in.shape[2]
    width = wide // 2
    rank = eigenvalues.shape[1]
    every = nb * rows
    half = every // 2
    members = nb // 2
    group, mine = lax.div(me, members), lax.rem(me, members)
    half_rank = rank // 4
    line = nb // 4
    px, py, pz = lax.rem(me, 2), lax.rem(lax.div(me, 2), 2), lax.div(me, 4)
    next_x = me + 1 - 2 * px
    next_y = me + 2 - 4 * py

    def span(index, size):
        return pl.ds(pl.multiple_of(index * size, size), size)

    def to_peer(source, target, send_sem, recv_sem, peer):
        return pltpu.make_async_remote_copy(
            src_ref=source, dst_ref=target, send_sem=send_sem, recv_sem=recv_sem,
            device_id={"blk": peer}, device_id_type=MESH,
        )

    def to_pair(source, target, index):
        return pltpu.make_async_remote_copy(
            src_ref=source, dst_ref=target,
            send_sem=pair_send.at[index], recv_sem=pair_recv.at[index],
            device_id={"col": 1 - side}, device_id_type=MESH,
        )

    def each_peer(body):
        def step(k, carry):
            body(lax.rem(me + k, nb))
            return carry
        lax.fori_loop(1, nb, step, 0)

    def each_member(body):
        def step(k, carry):
            body(lax.rem(mine + k, members))
            return carry
        lax.fori_loop(1, members, step, 0)

    def query_copy(source, peer):
        return to_peer(queries.at[:, span(lax.rem(peer, members), wide)], query_in.at[source],
                       query_send.at[peer], query_recv.at[source], peer)

    def factor_copy(source, member):
        return to_peer(factor_t.at[:, span(member, wide)], factor_in.at[source],
                       factor_send.at[member], factor_recv.at[source], group * members + member)

    def part_copy(source, member):
        return to_peer(part_sum.at[member], part_in.at[source],
                       part_send.at[member], part_recv.at[source], group * members + member)

    def scaled_copy(source, member):
        return to_peer(scaled_out, scaled_in.at[side, source],
                       scaled_send.at[member], scaled_recv.at[source], group * members + member)

    def cross_copy(k):
        return to_peer(cross_out.at[k], cross_in.at[k], cross_send.at[k], cross_recv.at[k],
                       (1 - group) * members + mine)

    def block(z, flip_x, flip_y):
        x = 1 - px if flip_x else px
        y = 1 - py if flip_y else py
        return z * 4 + y * 2 + x

    def line_copy(z, k, up):
        half_block = pre.at[block(z, False, False), pl.ds(k * half, half)]
        return to_peer(half_block, half_block, line_send.at[up, 2 * z + k],
                       line_recv.at[2 * z + k], me + (4 if up else -4))

    def side_copy(z, k, along, incoming=False):
        index = block(z, incoming and along == 0, incoming and along == 1)
        half_block = pre.at[index, pl.ds(k * half, half)]
        return to_peer(half_block, half_block, side_send.at[along, 2 * z + k],
                       side_recv.at[along, 2 * z + k], next_y if along else next_x)

    def corner_copy(z, along, incoming=False):
        index = block(z, incoming or along == 1, incoming or along == 0)
        half_block = pre.at[index, pl.ds((1 - along) * half, half)]
        return to_peer(half_block, half_block, corner_send.at[along, z],
                       corner_recv.at[along, z], next_y if along else next_x)

    def train_copy(index):
        chunk = lax.rem(index, members) * 2 + lax.div(index, members)
        return pltpu.make_async_copy(
            train_rows.at[:, span(chunk, width)], train_in.at[index], train_sem.at[index])

    own_query = pltpu.make_async_copy(
        queries.at[:, span(mine, wide)], query_in.at[me], own_sem.at[0])
    own_factor = pltpu.make_async_copy(
        factor_t.at[:, span(mine, wide)], factor_in.at[mine], own_sem.at[1])

    barrier = pltpu.get_barrier_semaphore()
    each_peer(lambda peer: pl.semaphore_signal(
        barrier, inc=1, device_id={"blk": peer}, device_id_type=MESH))
    pl.semaphore_signal(barrier, inc=1, device_id={"col": 1 - side}, device_id_type=MESH)
    pl.semaphore_wait(barrier, nb)

    own_query.start()
    own_factor.start()
    each_peer(lambda peer: query_copy(me, peer).start())
    each_member(lambda peer: factor_copy(mine, peer).start())

    def start_train(k, carry):
        train_copy(lax.rem(me + nb - k, nb)).start()
        return carry
    lax.fori_loop(0, nb, start_train, 0)

    own_query.wait()
    own_factor.wait()
    each_peer(lambda peer: query_copy(peer, peer).wait_recv())
    each_member(lambda peer: factor_copy(peer, peer).wait_recv())

    query_wide = query_in[...].astype(jnp.float32).reshape(every, wide)
    partial_value = lax.dot_general(
        query_wide.astype(jnp.bfloat16), factor_in[...].reshape(2 * half_rank, wide),
        CONTRACT_LAST, preferred_element_type=jnp.float32)
    for k in range(2):
        part[k] = partial_value[:, k * half_rank:(k + 1) * half_rank].reshape(
            members, 2 * rows, half_rank)

    exchange = to_pair(part.at[1 - side], pair_in, 0)
    exchange.start()
    own_rank = span(2 * group + side, half_rank)
    own_values = eigenvalues[:, own_rank]
    weights = own_values / (own_values + damping[0])
    exchange.wait()
    part_sum[...] = part[side] + pair_in[...]
    each_member(lambda peer: part_copy(mine, peer).start())
    part_in[mine] = part_sum[mine]
    each_member(lambda peer: part_copy(peer, peer).wait_recv())
    scaled_out[...] = jnp.sum(part_in[...], axis=0) * weights
    each_member(lambda peer: scaled_copy(mine, peer).start())
    scaled_in[side, mine] = scaled_out[...]
    each_member(lambda peer: scaled_copy(peer, peer).wait_recv())
    swap = to_pair(scaled_in.at[side], scaled_in.at[side], 2)
    swap.start()

    def correction_of(which, where):
        scaled = scaled_in[which].reshape(every, half_rank)
        first = scaled.astype(jnp.bfloat16)
        rest = scaled - first.astype(jnp.float32)
        second = rest.astype(jnp.bfloat16)
        third = (rest - second.astype(jnp.float32)).astype(jnp.bfloat16)
        slots = members // 2
        factor_half = factor_in[pl.ds(which * slots, slots), :, span(where, width)].reshape(
            half_rank, width)
        return (
            jnp.dot(third, factor_half, preferred_element_type=jnp.float32)
            + jnp.dot(second, factor_half, preferred_element_type=jnp.float32)
        ) + jnp.dot(first, factor_half, preferred_element_type=jnp.float32)

    outgoing = correction_of(side, 1 - group)
    swap.wait()
    outgoing = outgoing + correction_of(1 - side, 1 - group)
    cross_out[...] = outgoing.reshape(2, half, width)
    for k in range(2):
        cross_copy(k).start()
    correction = correction_of(side, group) + correction_of(1 - side, group)
    query_own = query_in[:, :, span(group, width)].astype(jnp.float32).reshape(every, width)

    def finish_own(k):
        cross_copy(k).wait_recv()
        rows_of = slice(k * half, (k + 1) * half)
        whole = correction[rows_of] + cross_in[k]
        pre[me, rows_of] = ((query_own[rows_of] - whole) / damping[0]).astype(jnp.bfloat16)

    def scores_of(index):
        train_copy(index).wait()
        return lax.dot_general(
            pre[index], train_in[index], CONTRACT_LAST, preferred_element_type=jnp.float32)

    def height(i):
        mirror = lax.div(pz, line // 2)
        near = pz + mirror * (line - 1 - 2 * pz)
        v = near + i * (1 - 2 * near) if i < 2 else i
        return v + mirror * (line - 1 - 2 * v)

    def pass_on(z, k):
        @pl.when((z <= pz) & (pz < line - 1))
        def _():
            line_copy(z, k, 1).start()

        @pl.when((z >= pz) & (pz > 0))
        def _():
            line_copy(z, k, 0).start()

    total[...] = jnp.zeros_like(total)
    for e in range(2 * line + 2):
        if e < 2 * line:
            i, k = divmod(e, 2)
            z = height(i)
            if i > 0:
                line_copy(z, k, 1).wait_recv()
            else:
                finish_own(k)
            pass_on(z, k)
            side_copy(z, k, 0).start()
            side_copy(z, k, 1).start()
        if 1 <= e <= 2 * line:
            i, k = divmod(e - 1, 2)
            z = height(i)
            side_copy(z, k, 0, True).wait_recv()
            if k == 0:
                corner_copy(z, 1).start()
            side_copy(z, k, 1, True).wait_recv()
            if k == 1:
                corner_copy(z, 0).start()
        if e >= 2:
            i, k = divmod(e - 2, 2)
            z = height(i)
            corner_copy(z, 1 - k, True).wait_recv()
            if k == 1:
                for flip_x in (False, True):
                    for flip_y in (False, True):
                        total[...] += scores_of(block(z, flip_x, flip_y))

    other_rows = pl.ds(pl.multiple_of((1 - side) * half, half), half)
    own_rows = pl.ds(pl.multiple_of(side * half, half), half)
    last = to_pair(total.at[other_rows], total_in, 1)
    last.start()

    each_peer(lambda peer: query_copy(me, peer).wait_send())

    def finish(peer):
        factor_copy(mine, peer).wait_send()
        part_copy(mine, peer).wait_send()
        scaled_copy(mine, peer).wait_send()
    each_member(finish)
    for k in range(2):
        cross_copy(k).wait_send()
    for i in range(line):
        z = height(i)
        for k in range(2):
            @pl.when((z <= pz) & (pz < line - 1))
            def _():
                line_copy(z, k, 1).wait_send()

            @pl.when((z >= pz) & (pz > 0))
            def _():
                line_copy(z, k, 0).wait_send()

            for along in range(2):
                side_copy(z, k, along).wait_send()
        for along in range(2):
            corner_copy(z, along).wait_send()
    last.wait()
    out[...] = (total[own_rows, :] + total_in[...]).astype(out.dtype)


def fused(nb, queries, factor, eigenvalues, damping, train_rows):
    rows, depth = queries.shape
    rank_slice = factor.shape[1]
    width = depth // nb
    rank = eigenvalues.shape[0]
    every = nb * rows
    train = train_rows.shape[0]
    line = nb // 4
    members = nb // 2
    anywhere = pl.BlockSpec(memory_space=pl.ANY)
    vmem = pl.BlockSpec(memory_space=pltpu.VMEM)
    dma = pltpu.SemaphoreType.DMA
    f32, bf16 = jnp.float32, jnp.bfloat16
    return pl.pallas_call(
        functools.partial(fused_kernel, nb),
        out_shape=jax.ShapeDtypeStruct((every // 2, train), bf16),
        in_specs=[anywhere, anywhere, vmem, pl.BlockSpec(memory_space=pltpu.SMEM), anywhere],
        out_specs=vmem,
        scratch_shapes=[
            pltpu.VMEM((nb, rows, 2 * width), bf16),
            pltpu.VMEM((members, rank_slice, 2 * width), bf16),
            pltpu.VMEM((nb, train, width), bf16),
            pltpu.VMEM((2, members, 2 * rows, rank // 4), f32),
            pltpu.VMEM((members, 2 * rows, rank // 4), f32),
            pltpu.VMEM((members, 2 * rows, rank // 4), f32),
            pltpu.VMEM((members, 2 * rows, rank // 4), f32),
            pltpu.VMEM((2 * rows, rank // 4), f32),
            pltpu.VMEM((2, members, 2 * rows, rank // 4), f32),
            pltpu.VMEM((2, every // 2, width), f32),
            pltpu.VMEM((2, every // 2, width), f32),
            pltpu.VMEM((nb, every, width), bf16),
            pltpu.VMEM((every, train), f32),
            pltpu.VMEM((every // 2, train), f32),
            dma((nb,)), dma((2,)),
            dma((nb,)), dma((nb,)), dma((members,)), dma((members,)),
            dma((members,)), dma((members,)), dma((members,)), dma((members,)),
            dma((2, 2 * line)), dma((2 * line,)), dma((2, 2 * line)), dma((2, 2 * line)),
            dma((2, line)), dma((2, line)), dma((3,)), dma((3,)), dma((2,)), dma((2,)),
        ],
        compiler_params=pltpu.CompilerParams(
            collective_id=0, has_side_effects=True, vmem_limit_bytes=56 * 1024 * 1024),
    )(queries, factor.T, eigenvalues[None, :], damping, train_rows)


def plain(queries, factor, eigenvalues, damping, train_rows):
    damp_value = damping[0]
    weights = eigenvalues / (eigenvalues + damp_value)
    query_part = lax.all_to_all(queries, "blk", split_axis=1, concat_axis=0, tiled=True)
    factor_part = lax.all_to_all(factor, "blk", split_axis=0, concat_axis=1, tiled=True)
    partial_value = jnp.dot(query_part, factor_part, preferred_element_type=jnp.float32)
    coefficient = lax.psum(partial_value, ("blk", "col"))
    scaled = coefficient * weights[None, :]
    correction = jnp.dot(scaled, factor_part.astype(jnp.float32).T, precision=lax.Precision.HIGHEST)
    pre_part = ((query_part.astype(jnp.float32) - correction) / damp_value).astype(jnp.bfloat16)
    pre_all = lax.all_gather(pre_part, "blk", axis=1, tiled=True)
    partial_scores = jnp.einsum("qk,nk->qn", pre_all, train_rows, preferred_element_type=jnp.float32)
    scores = lax.psum_scatter(partial_scores, "col", scatter_dimension=0, tiled=True)
    return scores.astype(jnp.bfloat16)


def per_device(nb, pair, queries, factor, eigenvalues, damping, train_rows):
    rows, depth = queries.shape
    width = depth // nb
    fits = pair == 2 and width % 128 == 0 and eigenvalues.shape[0] % 512 == 0 and rows % 8 == 0 and factor.shape[1] % 16 == 0
    fits = fits and nb == 16
    if fits:
        return fused(nb, queries, factor, eigenvalues, damping, train_rows)
    return plain(queries, factor, eigenvalues, damping, train_rows)


def solution(mesh):
    in_specs = (P("blk", "col"), P("col", "blk"), P(), P(), P("blk", "col"))
    out_specs = P("col", "blk")
    body = functools.partial(per_device, mesh.shape["blk"], mesh.shape["col"])
    return jax.shard_map(
        body, mesh=mesh, in_specs=in_specs, out_specs=out_specs, check_vma=False
    )
```

time: 87.2 us -> 82.6 us (0.947)
  Pallas kernels: 84.7 us -> 80.1 us
    pallas_call x1, Pallas kernels: 84.7 us -> 80.1 us  [fused(): pl.pallas_call(functools.partial(fused_kernel, nb), out_shape=jax.ShapeDt...]
where the time goes in v4:
time: 82.6 us; the launch traced here: 82.3 us
  Pallas kernels  80.1 us (97%)
  local copies, waits for them, and re-layouts  1.57 us (2%)
    pallas_call x1, Pallas kernels, fused(): pl.pallas_call(functools.partial(fused_kernel, nb), out_shape=jax.ShapeDt...  80.1 us

profile of v4, /device:TPU:0, one launch (start us, length us, event | category | flops | bytes accessed | tf_op | source)
XLA Modules:
  0.0 82.3 jit_solution(16263974196288267329)
XLA Ops:
  0.7 80.1 %shard_map.55 = bf16[64,1024]{1,0:T(8,128)(2,1)} custom-call(bf16[8,8192]{1,0:T(8,128)(2,1)} %queries.1, bf16[64,8192]{1,0:T(8,128)(2,1)} %bitcast.2, f32[1,1024]{1,0:T(1,128)} %bitcast.3, f32[1]{0:T(128)S(6)} %copy.7.damping, bf16[1024,8192]{1,0:T(8,128)(2,1)} %train_rows.1), custom_call_target="tpu_custom_call" | custom-call | tf_op jit(solution)/shard_map/pallas_call | solution.py:288
  80.7 1.6 %copy.8 = bf16[64,1024]{1,0:T(8,128)(2,1)} copy(bf16[64,1024]{1,0:T(8,128)(2,1)} %shard_map.55) | data formatting | bytes 262144

commit v5 on v4

--- a/solution.py
+++ b/solution.py
@@ -58,7 +58,7 @@
 
     def each_member(body):
         def step(k, carry):
-            body(lax.rem(mine + k, members))
+            body(mine + (k % 2) * (1 - 2 * lax.rem(mine, 2)) + 2 * (lax.rem(lax.div(k, 2), 2)) * (1 - 2 * lax.rem(lax.div(mine, 2), 2)) + 4 * lax.div(k, 4) * (1 - 2 * lax.div(mine, 4)))
             return carry
         lax.fori_loop(1, members, step, 0)
 
@@ -210,7 +210,12 @@
             line_copy(z, k, 0).start()
 
     total[...] = jnp.zeros_like(total)
-    for e in range(2 * line + 2):
+    side_lag, corner_lag = 3, 6
+
+    def add_scores(z, flip_x, flip_y):
+        total[...] += scores_of(block(z, flip_x, flip_y))
+
+    for e in range(2 * line + corner_lag):
         if e < 2 * line:
             i, k = divmod(e, 2)
             z = height(i)
@@ -221,23 +226,24 @@
             pass_on(z, k)
             side_copy(z, k, 0).start()
             side_copy(z, k, 1).start()
-        if 1 <= e <= 2 * line:
-            i, k = divmod(e - 1, 2)
+        if 0 <= e - side_lag < 2 * line:
+            i, k = divmod(e - side_lag, 2)
             z = height(i)
-            side_copy(z, k, 0, True).wait_recv()
-            if k == 0:
-                corner_copy(z, 1).start()
-            side_copy(z, k, 1, True).wait_recv()
+            side_copy(z, k, k, True).wait_recv()
+            corner_copy(z, 1 - k).start()
             if k == 1:
-                corner_copy(z, 0).start()
-        if e >= 2:
-            i, k = divmod(e - 2, 2)
+                side_copy(z, 1, 0, True).wait_recv()
+                add_scores(z, True, False)
+                side_copy(z, 0, 1, True).wait_recv()
+                add_scores(z, False, True)
+        if e < 2 * line and e % 2 == 1:
+            add_scores(height(e // 2), False, False)
+        if e >= corner_lag:
+            i, k = divmod(e - corner_lag, 2)
             z = height(i)
             corner_copy(z, 1 - k, True).wait_recv()
             if k == 1:
-                for flip_x in (False, True):
-                    for flip_y in (False, True):
-                        total[...] += scores_of(block(z, flip_x, flip_y))
+                add_scores(z, True, True)
 
     other_rows = pl.ds(pl.multiple_of((1 - side) * half, half), half)
     own_rows = pl.ds(pl.multiple_of(side * half, half), half)

time: 82.6 us -> 76.1 us (0.921)
  Pallas kernels: 80.1 us -> 73.6 us
    pallas_call x1, Pallas kernels: 80.1 us -> 73.6 us  [fused(): pl.pallas_call(functools.partial(fused_kernel, nb), out_shape=jax.ShapeDt...]
where the time goes in v5:
time: 76.1 us; the launch traced here: 75.8 us
  Pallas kernels  73.6 us (97%)
  local copies, waits for them, and re-layouts  1.57 us (2%)
    pallas_call x1, Pallas kernels, fused(): pl.pallas_call(functools.partial(fused_kernel, nb), out_shape=jax.ShapeDt...  73.6 us
    unnamed x1, local copies, waits for them, and re-layouts  1.57 us

profile of v5, /device:TPU:0, one launch (start us, length us, event | category | flops | bytes accessed | tf_op | source)
XLA Modules:
  0.0 75.8 jit_solution(5704314318139749437)
XLA Ops:
  0.7 73.6 %shard_map.55 = bf16[64,1024]{1,0:T(8,128)(2,1)} custom-call(bf16[8,8192]{1,0:T(8,128)(2,1)} %queries.1, bf16[64,8192]{1,0:T(8,128)(2,1)} %bitcast.2, f32[1,1024]{1,0:T(1,128)} %bitcast.3, f32[1]{0:T(128)S(6)} %copy.7.damping, bf16[1024,8192]{1,0:T(8,128)(2,1)} %train_rows.1), custom_call_target="tpu_custom_call" | custom-call | tf_op jit(solution)/shard_map/pallas_call | solution.py:294
  74.2 1.6 %copy.8 = bf16[64,1024]{1,0:T(8,128)(2,1)} copy(bf16[64,1024]{1,0:T(8,128)(2,1)} %shard_map.55) | data formatting | bytes 262144
